TPU v7x, 32 devices: a whole 2x2x4 slice. The times are simulated.
32 devices in a mesh: groups: 2 (over x), ctx: 8 (over z, y), head: 2 (over core).
Axes of the slice: x: 2, y: 2, z: 4, core: 2. Of those that a mesh axis runs over, the one named last changes fastest.
Arguments:
- queries: bfloat16 [4096, 2048], P(('groups', 'ctx'), 'head'), parts along dimension 0, may hold values from -180 to 180
- keys: bfloat16 [4096, 2048], P(('groups', 'ctx'), 'head'), parts along dimension 0, may hold values from -6 to 6
- values: bfloat16 [4096, 2048], P(('groups', 'ctx'), 'head'), parts along dimension 0, may hold values from -6 to 6
- out_weight: bfloat16 [2048, 2048], P(None, 'head'), may hold values from -0.125 to 0.125
- random_blocks: int32 [32, 3], P('groups'), parts along dimension 0, may hold values from 0 to 15, as said below
- window_blocks: int32 [32], P(('groups', 'ctx')), parts along dimension 0, may hold values from 0 to 1
- global_blocks: int32 [4], P('groups'), parts along dimension 0, may hold values from 0 to 15, as said below
Outputs:
- layer_out: bfloat16 [4096, 2048], P(('groups', 'ctx'), 'head'), parts along dimension 0
There are 2 independent parts, one for each index of `groups`. A program takes and returns all parts, laid end to end along the dimension named above; an argument that names none is the same for every part. Nothing has to cross between parts.
Inputs may be any that keep to these rules, and one draw needn't show every extreme that they name: `random_blocks`: the random blocks named in the rows of one index j of ctx (rows j * 2 to j * 2 + 1) lie outside blocks j * 2 to j * 2 + 1; counted with repeats, at most 1 of them lie in the blocks k * 2 to k * 2 + 1 of any one other index k, and exactly 1 for some k. `global_blocks`: 2 different block numbers.
All inputs are finite; a program needn't handle non-finite values.
Results may differ from a plain program's by a relative error of at most 0.0055.
Values may be sent and summed in bfloat16 or wider, within the bound.
A program may use at most 128 MiB of HBM per device.

v0:
```python
import math

import jax
import jax.numpy as jnp
from jax import lax
from jax.sharding import PartitionSpec as P

HEAD = 128
BLOCK = 128
WMAX = 1
GLOB = 2
RAND = 3


LARGE_NEG = -1e30


def with_halo(block, sides, width):
    for axis, dim in sides:
        count = lax.axis_size(axis)
        forward = [(i, i + 1) for i in range(count - 1)]
        backward = [(target, source) for source, target in forward]
        low = lax.ppermute(
            lax.slice_in_dim(block, block.shape[dim] - width, None, axis=dim), axis, forward
        )
        high = lax.ppermute(lax.slice_in_dim(block, 0, width, axis=dim), axis, backward)
        block = jnp.concatenate([low, block, high], axis=dim)
    return block


def split_heads(tensor):
    return tensor.reshape(tensor.shape[:-1] + (tensor.shape[-1] // HEAD, HEAD))


def block_partial(query_rows, key_rows, value_rows):
    query_heads = split_heads(query_rows)
    key_heads = split_heads(key_rows)
    value_heads = split_heads(value_rows)
    scores = jnp.einsum(
        "gqhd,gckhd->gchqk", query_heads, key_heads, preferred_element_type=jnp.float32
    ) * (1.0 / math.sqrt(HEAD))
    row_peak = jnp.max(scores, axis=-1)
    weights = jnp.exp(scores - row_peak[..., None])
    row_total = jnp.sum(weights, axis=-1)
    partial_out = jnp.einsum(
        "gchqk,gckhd->gcqhd",
        weights.astype(jnp.bfloat16),
        value_heads,
        preferred_element_type=jnp.float32,
    )
    partial_out = partial_out.reshape(partial_out.shape[:-2] + (-1,))
    return (partial_out, jnp.swapaxes(row_peak, -1, -2), jnp.swapaxes(row_total, -1, -2))


def combine(partial_out, row_peak, row_total, used_flags):
    used_mask = used_flags[:, :, None, None]
    best_peak = jnp.max(jnp.where(used_mask, row_peak, LARGE_NEG), axis=1, keepdims=True)
    factor = jnp.where(used_mask, jnp.exp(row_peak - best_peak), 0.0)
    weighted = jnp.sum(split_heads(partial_out) * factor[..., None], axis=1)
    normalizer = jnp.sum(row_total * factor, axis=1)
    result = weighted / normalizer[..., None]
    return result.reshape(result.shape[:-2] + (-1,))


def candidates(first_block, block_count, widths, global_ids, random_rows, total_blocks):
    query_ids = first_block + jnp.arange(block_count, dtype=jnp.int32)
    offsets = jnp.arange(-WMAX, WMAX + 1, dtype=jnp.int32)
    window_ids = query_ids[:, None] + offsets[None, :]
    window_valid = (
        (jnp.abs(offsets)[None, :] <= widths[:, None])
        & (window_ids >= 0)
        & (window_ids < total_blocks)
    )
    global_rows = jnp.broadcast_to(global_ids[None, :], (block_count, GLOB))
    block_ids = jnp.concatenate([window_ids, global_rows, random_rows], axis=1)
    valid = jnp.concatenate(
        [window_valid, jnp.ones((block_count, GLOB + RAND), dtype=bool)], axis=1
    )
    width_all = block_ids.shape[1]
    same_block = block_ids[:, :, None] == block_ids[:, None, :]
    earlier = jnp.arange(width_all)[None, :] < jnp.arange(width_all)[:, None]
    shadowed = jnp.any(same_block & valid[:, None, :] & earlier[None, :, :], axis=2)
    return (block_ids, valid & jnp.logical_not(shadowed))


def per_device(queries, keys, values, out_weight, random_blocks, window_blocks, global_blocks):
    ctx_count = lax.axis_size("ctx")
    position = lax.axis_index("ctx")
    tok_rows, row_width = queries.shape
    dev_blocks = tok_rows // BLOCK
    total_blocks = dev_blocks * ctx_count
    requests = dev_blocks * RAND
    capacity = (requests + ctx_count - 2) // (ctx_count - 1)
    first_block = position * dev_blocks
    key_value = jnp.stack([keys, values])
    own_blocks = key_value.reshape(2, dev_blocks, BLOCK, row_width)
    extended = with_halo(key_value, (("ctx", 1),), WMAX * BLOCK)
    rim_blocks = extended.reshape(2, dev_blocks + 2 * WMAX, BLOCK, row_width)
    global_owner = global_blocks // dev_blocks
    global_slot = global_blocks % dev_blocks
    picked = jnp.take(own_blocks, global_slot, axis=1)
    owned_here = (global_owner == position)[None, :, None, None]
    global_terms = jnp.where(owned_here, picked.astype(jnp.float32), 0.0)
    global_pairs = lax.psum(global_terms.astype(jnp.bfloat16), "ctx")
    request_table = random_blocks.reshape(ctx_count, requests)
    owners = request_table // dev_blocks
    within = request_table % dev_blocks
    same_owner = owners[:, :, None] == owners[:, None, :]
    before = jnp.arange(requests)[None, :] < jnp.arange(requests)[:, None]
    rank_table = jnp.sum(same_owner & before[None, :, :], axis=2)
    slot_ids = jnp.arange(capacity, dtype=jnp.int32)
    toward_me = (owners == position)[:, :, None] & (
        rank_table[:, :, None] == slot_ids[None, None, :]
    )
    send_index = jnp.sum(jnp.where(toward_me, within[:, :, None], 0), axis=1)
    my_owner = lax.dynamic_index_in_dim(owners, position, 0, keepdims=False)
    my_rank = lax.dynamic_index_in_dim(rank_table, position, 0, keepdims=False)
    my_slot = my_owner * capacity + my_rank
    my_random = lax.dynamic_slice_in_dim(random_blocks, first_block, dev_blocks, 0)
    block_ids, used_flags = candidates(
        first_block, dev_blocks, window_blocks, global_blocks, my_random, total_blocks
    )
    window_index = (
        jnp.arange(dev_blocks, dtype=jnp.int32)[:, None]
        + WMAX
        + jnp.arange(-WMAX, WMAX + 1, dtype=jnp.int32)[None, :]
    )
    global_index = jnp.broadcast_to(
        dev_blocks + 2 * WMAX + jnp.arange(GLOB, dtype=jnp.int32)[None, :], (dev_blocks, GLOB)
    )
    local_pool = jnp.concatenate([rim_blocks, global_pairs], axis=1)
    query_blocks = queries.reshape(dev_blocks, BLOCK, row_width)
    slot_hits = (my_owner[:, None, None] == jnp.arange(ctx_count)[None, :, None]) & (
        my_rank[:, None, None] == slot_ids[None, None, :]
    )
    query_pick = jnp.sum(
        jnp.where(slot_hits, (jnp.arange(requests) // RAND)[:, None, None], 0), axis=0
    )
    outgoing = jnp.take(query_blocks, query_pick, axis=0)
    arrived = lax.all_to_all(outgoing, "ctx", split_axis=0, concat_axis=0, tiled=True)
    item_rows = arrived.shape[2]
    partners = jnp.take(own_blocks, send_index, axis=1)
    flat_queries = arrived.reshape(ctx_count * capacity, item_rows, row_width)
    part_out, part_peak, part_total = block_partial(flat_queries, partners[0], partners[1])
    back_out = lax.all_to_all(part_out, "ctx", split_axis=0, concat_axis=0, tiled=True)
    back_peak = lax.all_to_all(part_peak, "ctx", split_axis=0, concat_axis=0, tiled=True)
    back_total = lax.all_to_all(part_total, "ctx", split_axis=0, concat_axis=0, tiled=True)
    head_count = back_peak.shape[-1]
    rand_out = back_out.reshape(ctx_count * capacity, BLOCK, row_width)[my_slot].reshape(
        dev_blocks, RAND, BLOCK, row_width
    )
    rand_peak = back_peak.reshape(ctx_count * capacity, BLOCK, head_count)[my_slot].reshape(
        dev_blocks, RAND, BLOCK, head_count
    )
    rand_total = back_total.reshape(ctx_count * capacity, BLOCK, head_count)[my_slot].reshape(
        dev_blocks, RAND, BLOCK, head_count
    )
    pool_index = jnp.concatenate([window_index, global_index], axis=1)
    remote_parts = (rand_out, rand_peak, rand_total)
    group_size = math.gcd(dev_blocks, max(1, 512 // BLOCK))
    steps_count = dev_blocks // group_size

    def regroup(tensor):
        return tensor.reshape((steps_count, group_size) + tensor.shape[1:])

    def attend(inputs):
        query_group, index_group, used_group, extra_group = inputs
        gathered = jnp.take(local_pool, index_group, axis=1)
        part_out, part_peak, part_total = block_partial(query_group, gathered[0], gathered[1])
        part_out = jnp.concatenate([part_out, extra_group[0]], axis=1)
        part_peak = jnp.concatenate([part_peak, extra_group[1]], axis=1)
        part_total = jnp.concatenate([part_total, extra_group[2]], axis=1)
        return combine(part_out, part_peak, part_total, used_group).astype(jnp.bfloat16)

    extra_groups = tuple((regroup(member) for member in remote_parts))
    attended = lax.map(
        attend, (regroup(query_blocks), regroup(pool_index), regroup(used_flags), extra_groups)
    )
    attended = attended.reshape(tok_rows, row_width)
    layer_sum = jnp.dot(
        lax.all_gather(attended, "head", axis=1, tiled=True),
        out_weight,
        preferred_element_type=jnp.float32,
    )
    return layer_sum.astype(jnp.bfloat16)


def solution(mesh):
    placed = (
        P(("groups", "ctx"), "head"),
        P(("groups", "ctx"), "head"),
        P(("groups", "ctx"), "head"),
        P(None, "head"),
        P("groups", None),
        P(("groups", "ctx")),
        P("groups"),
    )
    return jax.shard_map(
        per_device,
        mesh=mesh,
        in_specs=placed,
        out_specs=P(("groups", "ctx"), "head"),
        check_vma=False,
    )
```

profile of v0, /device:TPU:0, one launch (start us, length us, event | category | flops | bytes accessed | tf_op | source)
XLA Modules:
  0.0 301.7 jit_solution(17253878951724094730)
XLA Ops:
  6.6 0.8 copy.186
  7.6 0.2 convert_reduce_fusion
  7.8 0.2 add_reduce_fusion
  8.4 1.7 gather_fusion.3
  10.1 1.6 fusion.18
  11.7 7.3 %all-to-all-start = ((bf16[8,1,128,1024]{3,2,1,0:T(8,128)(2,1)}), bf16[8,1,128,1024]{3,2,1,0:T(8,128)(2,1)}, u32[]{:S(2)}, u32[]{:S(2)}) async-start(bf16[8,1,128,1024]{3,2,1,0:T(8,128)(2,1)} %fusion.18), calls=%async_computation | async-start | bytes 4194304 | tf_op jit(solution)/shard_map/all_to_all | solution.py:140
  19.7 2.7 gather_fusion.2
  22.5 2.7 bitcast_select_fusion
  25.1 1.8 fusion.48
  26.9 2.4 copy.198
  29.3 3.0 %copy.197 = bf16[1,8,1,128,1024]{3,4,1,2,0:T(8,128)(2,1)S(1)} copy(bf16[1,8,1,128,1024]{4,3,0,1,2:T(8,128)(2,1)} %get-tuple-element.41) | data formatting | bytes 4194304 | tf_op jit(solution)/shard_map/slice | solution.py:144
  32.4 35.0 %all-to-all-done = bf16[8,1,128,1024]{3,2,1,0:T(8,128)(2,1)} async-done(((bf16[8,1,128,1024]{3,2,1,0:T(8,128)(2,1)}), bf16[8,1,128,1024]{3,2,1,0:T(8,128)(2,1)}, u32[]{:S(2)}, u32[]{:S(2)}) %all-to-all-start) | async-done | bytes 2097184 | tf_op jit(solution)/shard_map/all_to_all | solution.py:140
  67.4 3.9 %copy.200 = bf16[8,1,128,1024]{2,3,0,1:T(8,128)(2,1)} copy(bf16[8,1,128,1024]{3,2,1,0:T(8,128)(2,1)} %all-to-all-done) | data formatting | bytes 4194304 | tf_op jit(solution)/shard_map/all_to_all | solution.py:140
  71.3 5.7 %bitcast_reduce_fusion.1 = (f32[8,8,128]{2,1,0:T(8,128)}, f32[8,8,128,128]{3,2,1,0:T(8,128)}) fusion(bf16[8,128,8,128]{1,3,2,0:T(8,128)(2,1)} %bitcast.118, bf16[8,128,8,128]{1,3,2,0:T(8,128)(2,1)} %bitcast.119), kind=kOutput, calls=%fused_computation.18 | convolution fusion | flops 270524416 | bytes 8421376 | tf_op jit(solution)/shard_map/gqhd,gckhd->gchqk/dot_general | solution.py:39
  77.0 3.6 %all-to-all-start.2 = ((f32[8,1,128,8]{2,3,1,0:T(8,128)}), f32[8,1,128,8]{2,3,1,0:T(8,128)S(1)}, u32[]{:S(2)}, u32[]{:S(2)}) async-start(f32[8,1,128,8]{2,3,1,0:T(8,128)} %bitcast.39), calls=%async_computation.2 | async-start | bytes 65536 | tf_op jit(solution)/shard_map/all_to_all | solution.py:146
  80.6 3.7 %fusion.6 = f32[8,8,128]{2,1,0:T(8,128)} fusion(f32[8,8,128,128]{3,2,1,0:T(8,128)} %get-tuple-element.49, f32[8,8,128]{2,1,0:T(8,128)} %get-tuple-element.48), kind=kLoop, calls=%fused_computation.20 | loop fusion | flops 3137536 | bytes 4259840 | tf_op jit(solution)/shard_map/reduce_sum | solution.py:44
  84.3 3.0 %all-to-all-done.2 = f32[8,1,128,8]{2,3,1,0:T(8,128)S(1)} async-done(((f32[8,1,128,8]{2,3,1,0:T(8,128)}), f32[8,1,128,8]{2,3,1,0:T(8,128)S(1)}, u32[]{:S(2)}, u32[]{:S(2)}) %all-to-all-start.2) | async-done | bytes 32800 | tf_op jit(solution)/shard_map/all_to_all | solution.py:146
  87.3 3.3 %all-to-all-start.3 = ((f32[8,1,128,8]{2,3,1,0:T(8,128)}), f32[8,1,128,8]{2,3,1,0:T(8,128)S(1)}, u32[]{:S(2)}, u32[]{:S(2)}) async-start(f32[8,1,128,8]{2,3,1,0:T(8,128)} %bitcast.44), calls=%async_computation.3 | async-start | bytes 65536 | tf_op jit(solution)/shard_map/all_to_all | solution.py:147
  90.6 5.1 %fusion.16 = f32[8,8,128,128]{3,2,1,0:T(8,128)} fusion(bf16[8,128,8,128]{1,3,2,0:T(8,128)(2,1)S(1)} %bitcast.116, f32[8,8,128,128]{3,2,1,0:T(8,128)} %get-tuple-element.49, f32[8,8,128]{2,1,0:T(8,128)} %get-tuple-element.48), kind=kOutput, calls=%fused_computation.29 | convolution fusion | flops 271581184 | bytes 10518528 | tf_op jit(solution)/shard_map/gchqk,gckhd->gcqhd/dot_general | solution.py:45
  95.8 1.5 all-to-all-done.3
  97.3 4.7 %all-to-all-start.1 = ((f32[8,1,128,1024]{2,3,1,0:T(8,128)}), f32[8,1,128,1024]{2,3,1,0:T(8,128)}, u32[]{:S(2)}, u32[]{:S(2)}) async-start(f32[8,1,128,1024]{2,3,1,0:T(8,128)} %bitcast.110), calls=%async_computation.1 | async-start | bytes 8388608 | tf_op jit(solution)/shard_map/all_to_all | solution.py:145
  102.1 1.6 gather_fusion
  103.7 2.5 fusion.24
  106.4 4.6 %collective-permute-start = (bf16[2,128,1024]{2,1,0:T(8,128)(2,1)S(1)}, bf16[2,128,1024]{2,1,0:T(8,128)(2,1)}, u32[]{:S(2)}, u32[]{:S(2)}) collective-permute-start(bf16[2,128,1024]{2,1,0:T(8,128)(2,1)S(1)} %get-tuple-element.42), channel_id=1, source_target_pairs={{0,2},{2,4},{4,6},{6,8},{8,10},{10,12},{12,14},{1,3},{3,5},{5,7},{... | collective-permute-start | bytes 1572872 | tf_op jit(solution)/shard_map/ppermute | solution.py:23
  111.0 1.5 collective-permute-start.1
  113.0 0.2 and_reduce_fusion
  113.4 0.8 bitcast_bitcast_fusion
  114.2 38.1 %collective-permute-done = bf16[2,128,1024]{2,1,0:T(8,128)(2,1)} collective-permute-done((bf16[2,128,1024]{2,1,0:T(8,128)(2,1)S(1)}, bf16[2,128,1024]{2,1,0:T(8,128)(2,1)}, u32[]{:S(2)}, u32[]{:S(2)}) %collective-permute-start) | collective-permute-done | bytes 524320 | tf_op jit(solution)/shard_map/ppermute | solution.py:23
  152.3 2.7 pad_maximum_fusion.1
  155.1 93.3 %all-reduce.3.cloned.1.call-done = bf16[2,2,128,1024]{3,2,0,1:T(8,128)(2,1)} async-done(((bf16[2,2,128,1024]{3,2,0,1:T(8,128)(2,1)}), bf16[2,2,128,1024]{3,2,0,1:T(8,128)(2,1)}) %all-reduce.3.cloned.1.call-update) | async-done | bytes 1048592 | tf_op jit(solution)/shard_map/psum | solution.py:104
  248.4 2.4 pad_maximum_fusion
  250.8 3.8 %gather_fusion.1 = bf16[10,2,128,1024]{3,2,1,0:T(8,128)(2,1)} fusion(bf16[2,6,128,1024]{3,2,1,0:T(8,128)(2,1)S(1)} %pad_maximum_fusion, s32[1024]{0:T(1024)S(1)} %pad_clamp_fusion.3), kind=kCustom, calls=%fused_computation.1 | custom fusion | bytes 10485800 | tf_op jit(solution)/shard_map/while/body/eval_jaxpr/jit(_take)/gather | solution.py:168
  254.6 8.0 %copy.182 = bf16[2,5,2,128,1024]{3,4,1,0,2:T(8,128)(2,1)} copy(bf16[2,5,2,128,1024]{4,3,2,1,0:T(8,128)(2,1)} %bitcast.109) | data formatting | bytes 10485760 | tf_op jit(solution)/shard_map/while/body/eval_jaxpr/jit(_take)/gather | solution.py:168
  262.6 3.1 %select_bitcast_fusion = bf16[2,2,5,128,1024]{3,4,2,1,0:T(8,128)(2,1)S(1)} fusion(bf16[2,5,2,128,1024]{3,4,1,0,2:T(8,128)(2,1)} %copy.182, pred[2,5]{1,0:T(4,128)(4,1)S(1)} %compare_and_fusion.4), kind=kLoop, calls=%fused_computation.13 | loop fusion | flops 2621440 | bytes 10485770 | tf_op jit(solution)/shard_map/while/body/eval_jaxpr/jit(_take)/select_n | solution.py:168
  265.7 0.4 fusion.47
  266.1 0.6 copy-done.5
  266.7 1.2 bitcast_reduce_fusion
  267.9 1.6 fusion.3
  269.5 3.2 %fusion.12 = f32[2,5,128,8,128]{2,4,3,1,0:T(8,128)} fusion(bf16[2,5,128,8,128]{2,4,3,1,0:T(8,128)(2,1)S(1)} %bitcast.114, bf16[2,5,8,128,128]{3,4,1,2,0:T(8,128)(2,1)S(1)} %get-tuple-element.26), kind=kOutput, calls=%fused_computation.27 | convolution fusion | flops 335544320 | bytes 10485760 | tf_op jit(solution)/shard_map/while/body/eval_jaxpr/gchqk,gckhd->gcqhd/dot_general | solution.py:45
  272.7 0.6 gather_fusion.5
  273.2 0.6 gather_fusion.6
  273.8 0.2 fusion.28
  274.1 2.9 gather_fusion.4
  277.0 3.2 %fusion.1 = f32[2,128,8,128]{1,3,2,0:T(8,128)S(1)} fusion(f32[2,3,128,8,128]{2,4,3,1,0:T(8,128)S(1)} %bitcast.113, f32[2,5,128,8,128]{2,4,3,1,0:T(8,128)} %fusion.12, f32[2,8,128,8]{2,3,1,0:T(8,128)S(1)} %copy.207), kind=kLoop, calls=%fused_computation.9 | loop fusion | flops 6029312 | bytes 9502720 | tf_op jit(solution)/shard_map/while/body/eval_jaxpr/reduce_sum | solution.py:59
  280.3 0.3 copy.209
  280.7 0.9 copy.237
  281.6 8.8 %all-gather.2.cloned.1.call-done = bf16[256,2048]{1,0:T(8,128)(2,1)} async-done(((bf16[256,1024]{1,0:T(8,128)(2,1)}), bf16[256,2048]{1,0:T(8,128)(2,1)}) %all-gather.2.cloned.1.call-update) | async-done | bytes 1048592 | tf_op jit(solution)/shard_map/all_gather | solution.py:181
  290.4 4.6 %convolution_convert_fusion = bf16[256,1024]{1,0:T(8,128)(2,1)} fusion(bf16[256,2048]{1,0:T(8,128)(2,1)} %all-gather.2.cloned.1.call-done, bf16[2048,1024]{1,0:T(8,128)(2,1)} %param.10), kind=kOutput, calls=%fused_computation.36 | convolution fusion | flops 1074003968 | bytes 5767168 | tf_op jit(solution)/shard_map/dot_general | solution.py:180
  (69 shorter events, 2.3 us)
Async XLA Ops:
  10.1 9.5 %copy-start.1 = (bf16[256,1024]{1,0:T(8,128)(2,1)S(1)}, bf16[256,1024]{1,0:T(8,128)(2,1)}, u32[]{:S(2)}) copy-start(bf16[256,1024]{1,0:T(8,128)(2,1)} %param.9) | copy-start | bytes 1572868
  10.1 9.5 %copy-start.3 = (bf16[256,1024]{1,0:T(8,128)(2,1)S(1)}, bf16[256,1024]{1,0:T(8,128)(2,1)}, u32[]{:S(2)}) copy-start(bf16[256,1024]{1,0:T(8,128)(2,1)} %param.8) | copy-start | bytes 1572868
  11.7 55.7 %all-to-all-start = ((bf16[8,1,128,1024]{3,2,1,0:T(8,128)(2,1)}), bf16[8,1,128,1024]{3,2,1,0:T(8,128)(2,1)}, u32[]{:S(2)}, u32[]{:S(2)}) async-start(bf16[8,1,128,1024]{3,2,1,0:T(8,128)(2,1)} %fusion.18), calls=%async_computation | async-start | bytes 4194304 | tf_op jit(solution)/shard_map/all_to_all | solution.py:140
  77.0 10.3 %all-to-all-start.2 = ((f32[8,1,128,8]{2,3,1,0:T(8,128)}), f32[8,1,128,8]{2,3,1,0:T(8,128)S(1)}, u32[]{:S(2)}, u32[]{:S(2)}) async-start(f32[8,1,128,8]{2,3,1,0:T(8,128)} %bitcast.39), calls=%async_computation.2 | async-start | bytes 65536 | tf_op jit(solution)/shard_map/all_to_all | solution.py:146
  87.3 10.0 %all-to-all-start.3 = ((f32[8,1,128,8]{2,3,1,0:T(8,128)}), f32[8,1,128,8]{2,3,1,0:T(8,128)S(1)}, u32[]{:S(2)}, u32[]{:S(2)}) async-start(f32[8,1,128,8]{2,3,1,0:T(8,128)} %bitcast.44), calls=%async_computation.3 | async-start | bytes 65536 | tf_op jit(solution)/shard_map/all_to_all | solution.py:147
  97.3 4.8 %copy-start.6 = (s32[2]{0:T(128)S(1)}, s32[2]{0:T(128)}, u32[]{:S(2)}) copy-start(s32[2]{0:T(128)} %param.13) | copy-start | bytes 28
  97.3 176.8 %all-to-all-start.1 = ((f32[8,1,128,1024]{2,3,1,0:T(8,128)}), f32[8,1,128,1024]{2,3,1,0:T(8,128)}, u32[]{:S(2)}, u32[]{:S(2)}) async-start(f32[8,1,128,1024]{2,3,1,0:T(8,128)} %bitcast.110), calls=%async_computation.1 | async-start | bytes 8388608 | tf_op jit(solution)/shard_map/all_to_all | solution.py:145
  102.0 4.4 %copy-start.2 = (bf16[256,1024]{1,0:T(8,128)(2,1)S(1)}, bf16[256,1024]{1,0:T(8,128)(2,1)}, u32[]{:S(2)}) copy-start(bf16[256,1024]{1,0:T(8,128)(2,1)} %param.9) | copy-start | bytes 1572868
  102.0 4.3 %copy-start.4 = (bf16[256,1024]{1,0:T(8,128)(2,1)S(1)}, bf16[256,1024]{1,0:T(8,128)(2,1)}, u32[]{:S(2)}) copy-start(bf16[256,1024]{1,0:T(8,128)(2,1)} %param.8) | copy-start | bytes 1572868
  102.0 10.8 %copy-start.7 = (s32[2]{0:T(128)S(1)}, s32[2]{0:T(128)}, u32[]{:S(2)}) copy-start(s32[2]{0:T(128)} %param.12) | copy-start | bytes 28
  102.0 11.3 %copy-start = (bf16[256,1024]{1,0:T(8,128)(2,1)S(1)}, bf16[256,1024]{1,0:T(8,128)(2,1)}, u32[]{:S(2)}) copy-start(bf16[256,1024]{1,0:T(8,128)(2,1)} %param.7) | copy-start | bytes 1572868
  102.0 146.3 %all-reduce.3.cloned.1.call-start = ((), (), s32[]{:S(2)}) async-start(), calls=%async_computation.4 | async-start | bytes 2097152 | tf_op jit(solution)/shard_map/psum | solution.py:104
  106.3 184.1 %all-gather.2.cloned.1.call-start = ((), (), s32[]{:S(2)}) async-start(), calls=%async_computation.5 | async-start | bytes 1572864 | tf_op jit(solution)/shard_map/all_gather | solution.py:181
  106.4 45.9 %collective-permute-start = (bf16[2,128,1024]{2,1,0:T(8,128)(2,1)S(1)}, bf16[2,128,1024]{2,1,0:T(8,128)(2,1)}, u32[]{:S(2)}, u32[]{:S(2)}) collective-permute-start(bf16[2,128,1024]{2,1,0:T(8,128)(2,1)S(1)} %get-tuple-element.42), channel_id=1, source_target_pairs={{0,2},{2,4},{4,6},{6,8},{8,10},{10,12},{12,14},{1,3},{3,5},{5,7},{... | collective-permute-start | bytes 1572872 | tf_op jit(solution)/shard_map/ppermute | solution.py:23
  111.0 41.3 %collective-permute-start.1 = (bf16[2,128,1024]{2,1,0:T(8,128)(2,1)S(1)}, bf16[2,128,1024]{2,1,0:T(8,128)(2,1)}, u32[]{:S(2)}, u32[]{:S(2)}) collective-permute-start(bf16[2,128,1024]{2,1,0:T(8,128)(2,1)S(1)} %get-tuple-element.43), channel_id=1, source_target_pairs={{2,0},{4,2},{6,4},{8,6},{10,8},{12,10},{14,12},{3,1},{5,3},{7,5},{... | collective-permute-start | bytes 1572872 | tf_op jit(solution)/shard_map/ppermute | solution.py:26
  265.7 1.0 copy-start.5
Sparse Core Ops, SparseCore 0:
  106.4 141.9 all-reduce.2
  281.7 8.6 all-gather.1
where the time goes:
time: 303 us; the launch traced here: 302 us
  waiting for transfers between devices  180 us (59%)
  local copies, waits for them, and re-layouts  37.8 us (12%)
  other arithmetic  25.6 us (8%)
  starting transfers between devices  25.1 us (8%)
  matrix products  19.7 us (7%)
  between operations  13.8 us (5%)
    psum x1, waiting for transfers between devices, per_device(): global_pairs = lax.psum(global_terms.astype(jnp.bfloat16), 'ctx')  93.3 us
    ppermute x1, waiting for transfers between devices, with_halo(): lax.ppermute(lax.slice_in_dim(block, block.shape[dim] - width, None, axis...  38.1 us
    all_to_all x1, waiting for transfers between devices, per_device(): lax.all_to_all(outgoing, 'ctx', split_axis=0, concat_axis=0, tiled=True)  35 us
    gather x2, local copies, waits for them, and re-layouts, attend(): gathered = jnp.take(local_pool, index_group, axis=1)  11.8 us
    all_gather x1, waiting for transfers between devices, per_device(): lax.all_gather(attended, 'head', axis=1, tiled=True)  8.78 us
    dot_general x2, matrix products, block_partial(): jnp.einsum('gchqk,gckhd->gcqhd', weights.astype(jnp.bfloat16), value_head...  8.28 us
    all_to_all x1, starting transfers between devices, per_device(): lax.all_to_all(outgoing, 'ctx', split_axis=0, concat_axis=0, tiled=True)  7.31 us
    dot_general x2, matrix products, block_partial(): jnp.einsum('gqhd,gckhd->gchqk', query_heads, key_heads, preferred_element...  6.82 us
  transfers between devices with their start and end apart: 8, of which 6 were waited for; matrix products, arithmetic and copies ran while one was open for 18% of the time, Pallas kernels for 0%

commit v1 on v0

v1 whole, which is shorter than its diff:
```python
import functools
import math

import jax
import jax.numpy as jnp
from jax import lax
from jax.experimental import pallas as pl
from jax.experimental.pallas import tpu as pltpu
from jax.sharding import PartitionSpec as P

HEAD = 128
BLOCK = 128
WMAX = 1
GLOB = 2
RAND = 3

LARGE_NEG = -1e30
MESH = pl.DeviceIdType.MESH

K_FWD, V_FWD, K_BWD, V_BWD = range(4)


def ring_place(index, count):
    odd = index % 2
    return (1 - odd) * (index // 2) + odd * (count - 1 - index // 2)


def ring_index(place, count):
    late = place // (count // 2)
    return (1 - late) * (2 * place) + late * (2 * (count - 1 - place) + 1)


def kernel(
    count,
    random_ref,
    window_ref,
    global_ref,
    q_hbm,
    k_hbm,
    v_hbm,
    w_hbm,
    out_ref,
    q_ref,
    w_ref,
    k_all,
    v_all,
    peak_ref,
    total_ref,
    acc_ref,
    own_ref,
    other_ref,
    sum_ref,
    load_sem,
    send_sem,
    recv_sem,
    pair_send,
    pair_recv,
):
    rows, width = q_ref.shape
    heads = width // HEAD
    dev_blocks = rows // BLOCK
    half = count // 2
    position = lax.axis_index("ctx")
    side = lax.axis_index("head")
    place = ring_place(position, count)
    right = ring_index((place + 1) % count, count)
    left = ring_index((place + count - 1) % count, count)

    load_k = pltpu.make_async_copy(k_hbm, k_all.at[0], load_sem.at[0])
    load_v = pltpu.make_async_copy(v_hbm, v_all.at[0], load_sem.at[1])
    load_q = pltpu.make_async_copy(q_hbm, q_ref, load_sem.at[2])
    load_w = pltpu.make_async_copy(w_hbm, w_ref, load_sem.at[3])
    load_k.start()
    load_v.start()
    load_q.start()

    barrier = pltpu.get_barrier_semaphore()
    pl.semaphore_signal(barrier, inc=1, device_id={"ctx": left}, device_id_type=MESH)
    pl.semaphore_signal(barrier, inc=1, device_id={"ctx": right}, device_id_type=MESH)
    pl.semaphore_signal(barrier, inc=1, device_id={"head": 1 - side}, device_id_type=MESH)
    pl.semaphore_wait(barrier, 3)

    def hop(stream, slot):
        buffer = k_all if stream in (K_FWD, K_BWD) else v_all
        forward = stream in (K_FWD, V_FWD)
        source = slot - 1 if forward else (slot + 1) % count
        return pltpu.make_async_remote_copy(
            src_ref=buffer.at[source],
            dst_ref=buffer.at[slot],
            send_sem=send_sem.at[stream, slot],
            recv_sem=recv_sem.at[stream, slot],
            device_id={"ctx": right if forward else left},
            device_id_type=MESH,
        )

    load_k.wait()
    hop(K_FWD, 1).start()
    hop(K_BWD, count - 1).start()
    load_v.wait()
    hop(V_FWD, 1).start()
    hop(V_BWD, count - 1).start()
    load_q.wait()
    load_w.start()

    peak_ref[...] = jnp.full_like(peak_ref, LARGE_NEG)
    total_ref[...] = jnp.zeros_like(total_ref)
    acc_ref[...] = jnp.zeros_like(acc_ref)
    scale = math.log2(math.e) / math.sqrt(HEAD)

    def use_bias(slot):
        owner = ring_index((place + count - slot) % count, count)
        query_rows = lax.broadcasted_iota(jnp.int32, (rows, rows), 0) // BLOCK
        key_cols = lax.broadcasted_iota(jnp.int32, (rows, rows), 1) // BLOCK
        bias = jnp.full((rows, rows), LARGE_NEG, jnp.float32)
        for a in range(dev_blocks):
            query_block = position * dev_blocks + a
            for b in range(dev_blocks):
                key_block = owner * dev_blocks + b
                offset = jnp.abs(key_block - query_block)
                used = (offset <= window_ref[a]) & (offset <= WMAX)
                for g in range(GLOB):
                    used = used | (global_ref[g] == key_block)
                for r in range(RAND):
                    used = used | (random_ref[query_block, r] == key_block)
                value = jnp.where(used, 0.0, LARGE_NEG)
                bias = jnp.where((query_rows == a) & (key_cols == b), value, bias)
        return bias

    def attend(slot):
        bias = use_bias(slot)

        def one_head(h, carry):
            cols = pl.ds(pl.multiple_of(h * HEAD, HEAD), HEAD)
            scores = lax.dot_general(
                q_ref[:, cols],
                k_all[slot, :, cols],
                (((1,), (1,)), ((), ())),
                preferred_element_type=jnp.float32,
            )
            scores = scores * scale + bias
            old_peak = peak_ref[h]
            new_peak = jnp.maximum(old_peak, jnp.max(scores, axis=1, keepdims=True))
            weights = jnp.exp2(scores - new_peak[:, :1])
            fade = jnp.exp2(old_peak - new_peak)
            part = jnp.dot(
                weights.astype(jnp.bfloat16),
                v_all[slot, :, cols],
                preferred_element_type=jnp.float32,
            )
            lanes = weights[:, :HEAD]
            for c in range(1, rows // HEAD):
                lanes = lanes + weights[:, c * HEAD : (c + 1) * HEAD]
            peak_ref[h] = new_peak
            total_ref[h] = total_ref[h] * fade + lanes
            acc_ref[h] = acc_ref[h] * fade + part
            return carry

        lax.fori_loop(0, heads, one_head, 0, unroll=2)

    def advance(step, last):
        back = count - step
        hop(K_FWD, step).wait_recv()
        hop(K_FWD, step + 1).start()
        hop(K_BWD, back).wait_recv()
        if not last:
            hop(K_BWD, back - 1).start()
        hop(V_BWD, back).wait_recv()
        hop(V_BWD, back - 1).start()
        hop(V_FWD, step).wait_recv()
        if not last:
            hop(V_FWD, step + 1).start()
        attend(step)
        attend(back)

    attend(0)

    def middle(step, carry):
        advance(step, False)
        return carry

    lax.fori_loop(1, half - 1, middle, 0)
    advance(half - 1, True)
    hop(K_FWD, half).wait_recv()
    hop(V_BWD, half).wait_recv()
    attend(half)

    for h in range(heads):
        total = jnp.sum(total_ref[h], axis=1, keepdims=True)
        own_ref[:, h * HEAD : (h + 1) * HEAD] = (acc_ref[h] / total).astype(jnp.bfloat16)

    exchange = pltpu.make_async_remote_copy(
        src_ref=own_ref,
        dst_ref=other_ref,
        send_sem=pair_send,
        recv_sem=pair_recv,
        device_id={"head": 1 - side},
        device_id_type=MESH,
    )
    exchange.start()
    load_w.wait()
    own_rows = pl.ds(pl.multiple_of(side * width, width), width)
    other_rows = pl.ds(pl.multiple_of((1 - side) * width, width), width)
    out_width = out_ref.shape[1]
    tile = min(256, out_width)

    def own_part(t, carry):
        cols = pl.ds(pl.multiple_of(t * tile, tile), tile)
        sum_ref[:, cols] = jnp.dot(
            own_ref[...], w_ref[own_rows, cols], preferred_element_type=jnp.float32
        )
        return carry

    lax.fori_loop(0, out_width // tile, own_part, 0)
    exchange.wait()

    def other_part(t, carry):
        cols = pl.ds(pl.multiple_of(t * tile, tile), tile)
        part = jnp.dot(
            other_ref[...], w_ref[other_rows, cols], preferred_element_type=jnp.float32
        )
        out_ref[:, cols] = (sum_ref[:, cols] + part).astype(out_ref.dtype)
        return carry

    lax.fori_loop(0, out_width // tile, other_part, 0)

    def drain(step, carry):
        hop(K_FWD, step).wait_send()
        hop(V_FWD, step).wait_send()
        hop(K_BWD, count - step).wait_send()
        hop(V_BWD, count - step).wait_send()
        return carry

    lax.fori_loop(1, half, drain, 0)
    hop(K_FWD, half).wait_send()
    hop(V_BWD, half).wait_send()


def per_device(queries, keys, values, out_weight, random_blocks, window_blocks, global_blocks):
    count = lax.axis_size("ctx")
    rows, width = queries.shape
    heads = width // HEAD
    out_width = out_weight.shape[1]
    smem = pl.BlockSpec(memory_space=pltpu.SMEM)
    hbm = pl.BlockSpec(memory_space=pl.ANY)
    return pl.pallas_call(
        functools.partial(kernel, count),
        out_shape=jax.ShapeDtypeStruct((rows, out_width), jnp.bfloat16),
        in_specs=[smem] * 3 + [hbm] * 4,
        out_specs=pl.BlockSpec(memory_space=pltpu.VMEM),
        scratch_shapes=[
            pltpu.VMEM((rows, width), jnp.bfloat16),
            pltpu.VMEM(out_weight.shape, jnp.bfloat16),
            pltpu.VMEM((count, rows, width), jnp.bfloat16),
            pltpu.VMEM((count, rows, width), jnp.bfloat16),
            pltpu.VMEM((heads, rows, HEAD), jnp.float32),
            pltpu.VMEM((heads, rows, HEAD), jnp.float32),
            pltpu.VMEM((heads, rows, HEAD), jnp.float32),
            pltpu.VMEM((rows, width), jnp.bfloat16),
            pltpu.VMEM((rows, width), jnp.bfloat16),
            pltpu.VMEM((rows, out_width), jnp.float32),
            pltpu.SemaphoreType.DMA((4,)),
            pltpu.SemaphoreType.DMA((4, count)),
            pltpu.SemaphoreType.DMA((4, count)),
            pltpu.SemaphoreType.DMA,
            pltpu.SemaphoreType.DMA,
        ],
        compiler_params=pltpu.CompilerParams(
            collective_id=0, has_side_effects=True, vmem_limit_bytes=60 * 1024 * 1024
        ),
    )(random_blocks, window_blocks, global_blocks, queries, keys, values, out_weight)


def solution(mesh):
    placed = (
        P(("groups", "ctx"), "head"),
        P(("groups", "ctx"), "head"),
        P(("groups", "ctx"), "head"),
        P(None, "head"),
        P("groups", None),
        P(("groups", "ctx")),
        P("groups"),
    )
    return jax.shard_map(
        per_device,
        mesh=mesh,
        in_specs=placed,
        out_specs=P(("groups", "ctx"), "head"),
        check_vma=False,
    )
```

time: 303 us -> 97.7 us (0.32)
  waiting for transfers between devices: 180 us -> 0 us
  Pallas kernels: 0 us -> 94.2 us
  local copies, waits for them, and re-layouts: 37.8 us -> 3.22 us
  other arithmetic: 25.6 us -> 0 us
  starting transfers between devices: 25.1 us -> 0 us
  matrix products: 19.7 us -> 0 us
  between operations: 13.8 us -> 0.01 us
    pallas_call x0 -> x1, Pallas kernels: none -> 94.2 us  [per_device(): pl.pallas_call(functools.partial(kernel, count), out_shape=jax.ShapeDtype...]
    psum x1 -> x0, waiting for transfers between devices: 93.3 us -> none  [per_device(): global_pairs = lax.psum(global_terms.astype(jnp.bfloat16), 'ctx')]
    all_to_all x4 -> x0, waiting for transfers between devices: 39.5 us -> none  [the longest x1 35 us: per_device(): lax.all_to_all(outgoing, 'ctx', split_axis=0, concat_axis=0, tiled=True)]
    ppermute x2 -> x0, waiting for transfers between devices: 38.1 us -> none  [the longest x1 38.1 us: with_halo(): lax.ppermute(lax.slice_in_dim(block, block.shape[dim] - width, None, axis...]
    gather x8 -> x0, local copies, waits for them, and re-layouts: 21.9 us -> none  [the longest x2 11.8 us: attend(): gathered = jnp.take(local_pool, index_group, axis=1)]
    dot_general x5 -> x0, matrix products: 19.7 us -> none  [the longest x2 8.28 us: block_partial(): jnp.einsum('gchqk,gckhd->gcqhd', weights.astype(jnp.bfloat16), value_head...]
    all_to_all x4 -> x0, starting transfers between devices: 19 us -> none  [the longest x1 7.31 us: per_device(): lax.all_to_all(outgoing, 'ctx', split_axis=0, concat_axis=0, tiled=True)]
    reduce_sum x7 -> x0, other arithmetic: 9.02 us -> none  [the longest x2 5.25 us: block_partial(): row_total = jnp.sum(weights, axis=-1)]
  transfers between devices with their start and end apart: 8 -> 0, of which waited for: 6 -> 0; matrix products, arithmetic and copies ran while one was open for 18% -> 0% of each run, Pallas kernels for 0% -> 0%
where the time goes in v1:
time: 97.7 us; the launch traced here: 97.5 us
  Pallas kernels  94.2 us (96%)
  local copies, waits for them, and re-layouts  3.22 us (3%)
    pallas_call x1, Pallas kernels, per_device(): pl.pallas_call(functools.partial(kernel, count), out_shape=jax.ShapeDtype...  94.2 us
    unnamed x2, local copies, waits for them, and re-layouts  3.22 us

profile of v1, /device:TPU:0, one launch (start us, length us, event | category | flops | bytes accessed | tf_op | source)
XLA Modules:
  0.0 97.5 jit_solution(15390606781689829444)
XLA Ops:
  0.0 1.4 %copy.8.random_ref = s32[16,3]{1,0:T(8,128)} copy(s32[16,3]{0,1:T(4,128)} %param.11) | data formatting | bytes 384 | tf_op args[4]
  1.4 94.2 %shard_map.73 = bf16[256,1024]{1,0:T(8,128)(2,1)} custom-call(s32[16,3]{1,0:T(8,128)} %copy.8.random_ref, s32[2]{0:T(128)} %window_ref.1, s32[2]{0:T(128)} %global_ref.1, bf16[256,1024]{1,0:T(8,128)(2,1)} %q_hbm.1, bf16[256,1024]{1,0:T(8,128)(2,1)} %k_hbm.1, bf16[256,1024]{1,0:T(8,128)(2,1)} %v_hbm.1, bf16[2048,1024]{1,0:T(8,128)(2,1)} %w_hbm.1), custom_call_target="tpu_custom_call" | custom-call | tf_op jit(solution)/shard_map/pallas_call | solution.py:245
  95.6 1.9 %copy.10 = bf16[256,1024]{1,0:T(8,128)(2,1)} copy(bf16[256,1024]{1,0:T(8,128)(2,1)} %shard_map.73) | data formatting | bytes 1048576

commit v2 on v1

--- a/solution.py
+++ b/solution.py
@@ -53,6 +53,8 @@
     load_sem,
     send_sem,
     recv_sem,
+    last_send,
+    last_recv,
     pair_send,
     pair_recv,
 ):
@@ -109,119 +111,155 @@
 
     def use_bias(slot):
         owner = ring_index((place + count - slot) % count, count)
-        query_rows = lax.broadcasted_iota(jnp.int32, (rows, rows), 0) // BLOCK
-        key_cols = lax.broadcasted_iota(jnp.int32, (rows, rows), 1) // BLOCK
-        bias = jnp.full((rows, rows), LARGE_NEG, jnp.float32)
-        for a in range(dev_blocks):
-            query_block = position * dev_blocks + a
-            for b in range(dev_blocks):
-                key_block = owner * dev_blocks + b
+        row_block = lax.broadcasted_iota(jnp.int32, (rows, HEAD), 0) // BLOCK
+        biases = []
+        for b in range(dev_blocks):
+            key_block = owner * dev_blocks + b
+            bias = jnp.full((rows, HEAD), LARGE_NEG, jnp.float32)
+            for a in range(dev_blocks):
+                query_block = position * dev_blocks + a
                 offset = jnp.abs(key_block - query_block)
                 used = (offset <= window_ref[a]) & (offset <= WMAX)
                 for g in range(GLOB):
                     used = used | (global_ref[g] == key_block)
                 for r in range(RAND):
                     used = used | (random_ref[query_block, r] == key_block)
-                value = jnp.where(used, 0.0, LARGE_NEG)
-                bias = jnp.where((query_rows == a) & (key_cols == b), value, bias)
-        return bias
-
-    def attend(slot):
-        bias = use_bias(slot)
-
-        def one_head(h, carry):
+                bias = jnp.where(row_block == a, jnp.where(used, 0.0, LARGE_NEG), bias)
+            biases.append(bias)
+        return biases
+
+    def attend_head(slot, h, biases):
+        cols = pl.ds(h * HEAD, HEAD)
+        if not isinstance(h, int):
             cols = pl.ds(pl.multiple_of(h * HEAD, HEAD), HEAD)
-            scores = lax.dot_general(
-                q_ref[:, cols],
-                k_all[slot, :, cols],
-                (((1,), (1,)), ((), ())),
+        scores = lax.dot_general(
+            q_ref[:, cols],
+            k_all[slot, :, cols],
+            (((1,), (1,)), ((), ())),
+            preferred_element_type=jnp.float32,
+        )
+        scores = scores * scale
+        old_peak = peak_ref[h]
+        best_peak = old_peak
+        parts = []
+        for b, bias in enumerate(biases):
+            block = scores[:, b * BLOCK : (b + 1) * BLOCK]
+            row_peak = jnp.max(block, axis=1, keepdims=True)
+            weights = jnp.exp2(block - row_peak)
+            part = jnp.dot(
+                weights.astype(jnp.bfloat16),
+                v_all[slot, b * BLOCK : (b + 1) * BLOCK, cols],
                 preferred_element_type=jnp.float32,
             )
-            scores = scores * scale + bias
-            old_peak = peak_ref[h]
-            new_peak = jnp.maximum(old_peak, jnp.max(scores, axis=1, keepdims=True))
-            weights = jnp.exp2(scores - new_peak[:, :1])
-            fade = jnp.exp2(old_peak - new_peak)
-            part = jnp.dot(
-                weights.astype(jnp.bfloat16),
-                v_all[slot, :, cols],
-                preferred_element_type=jnp.float32,
-            )
-            lanes = weights[:, :HEAD]
-            for c in range(1, rows // HEAD):
-                lanes = lanes + weights[:, c * HEAD : (c + 1) * HEAD]
-            peak_ref[h] = new_peak
-            total_ref[h] = total_ref[h] * fade + lanes
-            acc_ref[h] = acc_ref[h] * fade + part
+            used_peak = row_peak + bias
+            best_peak = jnp.maximum(best_peak, used_peak)
+            parts.append((used_peak, weights, part))
+        fade = jnp.exp2(old_peak - best_peak)
+        total = total_ref[h] * fade
+        acc = acc_ref[h] * fade
+        for used_peak, weights, part in parts:
+            factor = jnp.exp2(used_peak - best_peak)
+            total = total + weights * factor
+            acc = acc + part * factor
+        return best_peak, total, acc
+
+    def attend(slot):
+        biases = use_bias(slot)
+
+        def one_head(h, carry):
+            peak_ref[h], total_ref[h], acc_ref[h] = attend_head(slot, h, biases)
             return carry
 
         lax.fori_loop(0, heads, one_head, 0, unroll=2)
 
-    def advance(step, last):
+    def last_hop(stream, h):
+        buffer = k_all if stream == K_FWD else v_all
+        forward = h % 2 == 0
+        cols = pl.ds(h * HEAD, HEAD)
+        return pltpu.make_async_remote_copy(
+            src_ref=buffer.at[half - 1 if forward else half + 1, :, cols],
+            dst_ref=buffer.at[half, :, cols],
+            send_sem=last_send.at[stream, h],
+            recv_sem=last_recv.at[stream, h],
+            device_id={"ctx": right if forward else left},
+            device_id_type=MESH,
+        )
+
+    attend(0)
+
+    def middle(step, carry):
         back = count - step
         hop(K_FWD, step).wait_recv()
         hop(K_FWD, step + 1).start()
         hop(K_BWD, back).wait_recv()
-        if not last:
-            hop(K_BWD, back - 1).start()
+        hop(K_BWD, back - 1).start()
+        hop(V_FWD, step).wait_recv()
+        hop(V_FWD, step + 1).start()
         hop(V_BWD, back).wait_recv()
         hop(V_BWD, back - 1).start()
-        hop(V_FWD, step).wait_recv()
-        if not last:
-            hop(V_FWD, step + 1).start()
         attend(step)
         attend(back)
-
-    attend(0)
-
-    def middle(step, carry):
-        advance(step, False)
         return carry
 
     lax.fori_loop(1, half - 1, middle, 0)
-    advance(half - 1, True)
-    hop(K_FWD, half).wait_recv()
-    hop(V_BWD, half).wait_recv()
-    attend(half)
-
+
+    for side_of, key_stream in ((0, K_FWD), (1, K_BWD)):
+        hop(key_stream, half + 1 if side_of else half - 1).wait_recv()
+        for pair in range(min(2, heads // 2)):
+            last_hop(K_FWD, 2 * pair + side_of).start()
+    for side_of, value_stream in ((0, V_FWD), (1, V_BWD)):
+        hop(value_stream, half + 1 if side_of else half - 1).wait_recv()
+        for pair in range(heads // 2):
+            last_hop(V_FWD, 2 * pair + side_of).start()
+            if pair + 2 < heads // 2:
+                last_hop(K_FWD, 2 * (pair + 2) + side_of).start()
+    attend(half - 1)
+    attend(half + 1)
+    load_w.wait()
+    biases = use_bias(half)
+    group = 2 * HEAD
+
+    def exchange(g):
+        cols = pl.ds(g * group, group)
+        return pltpu.make_async_remote_copy(
+            src_ref=own_ref.at[:, cols],
+            dst_ref=other_ref.at[:, cols],
+            send_sem=pair_send.at[g],
+            recv_sem=pair_recv.at[g],
+            device_id={"head": 1 - side},
+            device_id_type=MESH,
+        )
+
+    def project(source, which, g):
+        w_rows = pl.ds(pl.multiple_of(which * width + g * group, group), group)
+        return jnp.dot(
+            source[:, g * group : (g + 1) * group],
+            w_ref[w_rows, :],
+            preferred_element_type=jnp.float32,
+        )
+
+    groups = width // group
+    for g in range(groups):
+        for h in (2 * g, 2 * g + 1):
+            last_hop(K_FWD, h).wait_recv()
+            last_hop(V_FWD, h).wait_recv()
+            _, total, acc = attend_head(half, h, biases)
+            total = jnp.sum(total, axis=1, keepdims=True)
+            own_ref[:, h * HEAD : (h + 1) * HEAD] = (acc / total).astype(jnp.bfloat16)
+        exchange(g).start()
+        if g == 0:
+            sum_ref[...] = project(own_ref, side, g)
+        else:
+            exchange(g - 1).wait_recv()
+            sum_ref[...] += project(other_ref, 1 - side, g - 1) + project(own_ref, side, g)
+    exchange(groups - 1).wait_recv()
+    out_ref[...] = (sum_ref[...] + project(other_ref, 1 - side, groups - 1)).astype(out_ref.dtype)
+
+    for g in range(groups):
+        exchange(g).wait_send()
     for h in range(heads):
-        total = jnp.sum(total_ref[h], axis=1, keepdims=True)
-        own_ref[:, h * HEAD : (h + 1) * HEAD] = (acc_ref[h] / total).astype(jnp.bfloat16)
-
-    exchange = pltpu.make_async_remote_copy(
-        src_ref=own_ref,
-        dst_ref=other_ref,
-        send_sem=pair_send,
-        recv_sem=pair_recv,
-        device_id={"head": 1 - side},
-        device_id_type=MESH,
-    )
-    exchange.start()
-    load_w.wait()
-    own_rows = pl.ds(pl.multiple_of(side * width, width), width)
-    other_rows = pl.ds(pl.multiple_of((1 - side) * width, width), width)
-    out_width = out_ref.shape[1]
-    tile = min(256, out_width)
-
-    def own_part(t, carry):
-        cols = pl.ds(pl.multiple_of(t * tile, tile), tile)
-        sum_ref[:, cols] = jnp.dot(
-            own_ref[...], w_ref[own_rows, cols], preferred_element_type=jnp.float32
-        )
-        return carry
-
-    lax.fori_loop(0, out_width // tile, own_part, 0)
-    exchange.wait()
-
-    def other_part(t, carry):
-        cols = pl.ds(pl.multiple_of(t * tile, tile), tile)
-        part = jnp.dot(
-            other_ref[...], w_ref[other_rows, cols], preferred_element_type=jnp.float32
-        )
-        out_ref[:, cols] = (sum_ref[:, cols] + part).astype(out_ref.dtype)
-        return carry
-
-    lax.fori_loop(0, out_width // tile, other_part, 0)
+        last_hop(K_FWD, h).wait_send()
+        last_hop(V_FWD, h).wait_send()
 
     def drain(step, carry):
         hop(K_FWD, step).wait_send()
@@ -231,8 +269,6 @@
         return carry
 
     lax.fori_loop(1, half, drain, 0)
-    hop(K_FWD, half).wait_send()
-    hop(V_BWD, half).wait_send()
 
 
 def per_device(queries, keys, values, out_weight, random_blocks, window_blocks, global_blocks):
@@ -261,8 +297,10 @@
             pltpu.SemaphoreType.DMA((4,)),
             pltpu.SemaphoreType.DMA((4, count)),
             pltpu.SemaphoreType.DMA((4, count)),
-            pltpu.SemaphoreType.DMA,
-            pltpu.SemaphoreType.DMA,
+            pltpu.SemaphoreType.DMA((2, heads)),
+            pltpu.SemaphoreType.DMA((2, heads)),
+            pltpu.SemaphoreType.DMA((heads // 2,)),
+            pltpu.SemaphoreType.DMA((heads // 2,)),
         ],
         compiler_params=pltpu.CompilerParams(
             collective_id=0, has_side_effects=True, vmem_limit_bytes=60 * 1024 * 1024

time: 97.7 us -> 92.5 us (0.947)
  Pallas kernels: 94.2 us -> 88.9 us
    pallas_call x1, Pallas kernels: 94.2 us -> 88.9 us  [per_device(): pl.pallas_call(functools.partial(kernel, count), out_shape=jax.ShapeDtype...]
where the time goes in v2:
time: 92.5 us; the launch traced here: 92.1 us
  Pallas kernels  88.9 us (96%)
  local copies, waits for them, and re-layouts  3.22 us (3%)
    pallas_call x1, Pallas kernels, per_device(): pl.pallas_call(functools.partial(kernel, count), out_shape=jax.ShapeDtype...  88.9 us
    unnamed x2, local copies, waits for them, and re-layouts  3.22 us

profile of v2, /device:TPU:0, one launch (start us, length us, event | category | flops | bytes accessed | tf_op | source)
XLA Modules:
  0.0 92.1 jit_solution(6878533414824284563)
XLA Ops:
  0.0 1.4 %copy.8.random_ref = s32[16,3]{1,0:T(8,128)} copy(s32[16,3]{0,1:T(4,128)} %param.11) | data formatting | bytes 384 | tf_op args[4]
  1.4 88.9 %shard_map.73 = bf16[256,1024]{1,0:T(8,128)(2,1)} custom-call(s32[16,3]{1,0:T(8,128)} %copy.8.random_ref, s32[2]{0:T(128)} %window_ref.1, s32[2]{0:T(128)} %global_ref.1, bf16[256,1024]{1,0:T(8,128)(2,1)} %q_hbm.1, bf16[256,1024]{1,0:T(8,128)(2,1)} %k_hbm.1, bf16[256,1024]{1,0:T(8,128)(2,1)} %v_hbm.1, bf16[2048,1024]{1,0:T(8,128)(2,1)} %w_hbm.1), custom_call_target="tpu_custom_call" | custom-call | tf_op jit(solution)/shard_map/pallas_call | solution.py:281
  90.2 1.9 %copy.10 = bf16[256,1024]{1,0:T(8,128)(2,1)} copy(bf16[256,1024]{1,0:T(8,128)(2,1)} %shard_map.73) | data formatting | bytes 1048576

commit v3 on v2

--- a/solution.py
+++ b/solution.py
@@ -39,7 +39,7 @@
     k_hbm,
     v_hbm,
     w_hbm,
-    out_ref,
+    out_any,
     q_ref,
     w_ref,
     k_all,
@@ -50,6 +50,7 @@
     own_ref,
     other_ref,
     sum_ref,
+    out_ref,
     load_sem,
     send_sem,
     recv_sem,
@@ -123,7 +124,7 @@
                 for g in range(GLOB):
                     used = used | (global_ref[g] == key_block)
                 for r in range(RAND):
-                    used = used | (random_ref[query_block, r] == key_block)
+                    used = used | (random_ref[r, query_block] == key_block)
                 bias = jnp.where(row_block == a, jnp.where(used, 0.0, LARGE_NEG), bias)
             biases.append(bias)
         return biases
@@ -255,6 +256,8 @@
     exchange(groups - 1).wait_recv()
     out_ref[...] = (sum_ref[...] + project(other_ref, 1 - side, groups - 1)).astype(out_ref.dtype)
 
+    store = pltpu.make_async_copy(out_ref, out_any, load_sem.at[4])
+    store.start()
     for g in range(groups):
         exchange(g).wait_send()
     for h in range(heads):
@@ -269,6 +272,7 @@
         return carry
 
     lax.fori_loop(1, half, drain, 0)
+    store.wait()
 
 
 def per_device(queries, keys, values, out_weight, random_blocks, window_blocks, global_blocks):
@@ -277,12 +281,12 @@
     heads = width // HEAD
     out_width = out_weight.shape[1]
     smem = pl.BlockSpec(memory_space=pltpu.SMEM)
-    hbm = pl.BlockSpec(memory_space=pl.ANY)
+    hbm = pl.BlockSpec(memory_space=pltpu.HBM)
     return pl.pallas_call(
         functools.partial(kernel, count),
         out_shape=jax.ShapeDtypeStruct((rows, out_width), jnp.bfloat16),
         in_specs=[smem] * 3 + [hbm] * 4,
-        out_specs=pl.BlockSpec(memory_space=pltpu.VMEM),
+        out_specs=pl.BlockSpec(memory_space=pl.ANY),
         scratch_shapes=[
             pltpu.VMEM((rows, width), jnp.bfloat16),
             pltpu.VMEM(out_weight.shape, jnp.bfloat16),
@@ -294,7 +298,8 @@
             pltpu.VMEM((rows, width), jnp.bfloat16),
             pltpu.VMEM((rows, width), jnp.bfloat16),
             pltpu.VMEM((rows, out_width), jnp.float32),
-            pltpu.SemaphoreType.DMA((4,)),
+            pltpu.VMEM((rows, out_width), jnp.bfloat16),
+            pltpu.SemaphoreType.DMA((5,)),
             pltpu.SemaphoreType.DMA((4, count)),
             pltpu.SemaphoreType.DMA((4, count)),
             pltpu.SemaphoreType.DMA((2, heads)),
@@ -303,9 +308,9 @@
             pltpu.SemaphoreType.DMA((heads // 2,)),
         ],
         compiler_params=pltpu.CompilerParams(
-            collective_id=0, has_side_effects=True, vmem_limit_bytes=60 * 1024 * 1024
+            collective_id=0, has_side_effects=True, vmem_limit_bytes=60 << 20
         ),
-    )(random_blocks, window_blocks, global_blocks, queries, keys, values, out_weight)
+    )(random_blocks.T, window_blocks, global_blocks, queries, keys, values, out_weight)
 
 
 def solution(mesh):

time: 92.5 us -> 91 us (0.984)
  local copies, waits for them, and re-layouts: 3.22 us -> 1.87 us
    unnamed x2 -> x1, local copies, waits for them, and re-layouts: 3.22 us -> 1.87 us
where the time goes in v3:
time: 91 us; the launch traced here: 90.4 us
  Pallas kernels  88.5 us (97%)
  local copies, waits for them, and re-layouts  1.87 us (2%)
    pallas_call x1, Pallas kernels, per_device(): pl.pallas_call(functools.partial(kernel, count), out_shape=jax.ShapeDtype...  88.5 us
    unnamed x1, local copies, waits for them, and re-layouts  1.87 us

profile of v3, /device:TPU:0, one launch (start us, length us, event | category | flops | bytes accessed | tf_op | source)
XLA Modules:
  0.0 90.4 jit_solution(4073773883197362615)
XLA Ops:
  0.0 88.5 %shard_map.73 = bf16[256,1024]{1,0:T(8,128)(2,1)} custom-call(s32[3,16]{1,0:T(4,128)} %bitcast.1, s32[2]{0:T(128)} %window_ref.1, s32[2]{0:T(128)} %global_ref.1, bf16[256,1024]{1,0:T(8,128)(2,1)} %q_hbm.1, bf16[256,1024]{1,0:T(8,128)(2,1)} %k_hbm.1, bf16[256,1024]{1,0:T(8,128)(2,1)} %v_hbm.1, bf16[2048,1024]{1,0:T(8,128)(2,1)} %w_hbm.1), custom_call_target="tpu_custom_call" | custom-call | tf_op jit(solution)/shard_map/pallas_call | solution.py:285
  88.5 1.9 %copy.9 = bf16[256,1024]{1,0:T(8,128)(2,1)} copy(bf16[256,1024]{1,0:T(8,128)(2,1)} %shard_map.73) | data formatting | bytes 1048576
